TPU v7x, 32 devices: a whole 2x2x4 slice. The times are simulated.
32 devices in a mesh: dp: 16 (over z, x, core), tensor: 2 (over y).
Axes of the slice: x: 2, y: 2, z: 4, core: 2. Of those that a mesh axis runs over, the one named last changes fastest.
Arguments:
- inputs: float32 [16, 256, 768], P('dp'), may hold values from -6 to 6
- condition: float32 [16, 768], P('dp'), may hold values from -2.5 to 2.5
- cotangent: float32 [16, 256, 768], P('dp'), may hold values from -6 to 6
- w_qkv: float32 [2, 768, 3, 768], P(None, None, None, 'tensor'), may hold values from -0.21875 to 0.21875
- b_qv: float32 [2, 2, 768], P(None, None, 'tensor'), may hold values from -1.25 to 1.25
- w_out: float32 [2, 768, 768], P(None, 'tensor'), may hold values from -0.875 to 0.875
- b_out: float32 [2, 768], replicated, may hold values from -3 to 3
- w_up: float32 [2, 768, 3072], P(None, None, 'tensor'), may hold values from -0.21875 to 0.21875
- b_up: float32 [2, 3072], P(None, 'tensor'), may hold values from -3 to 3
- w_down: float32 [2, 3072, 768], P(None, 'tensor'), may hold values from -0.109375 to 0.109375
- b_down: float32 [2, 768], replicated, may hold values from -3 to 3
- w_mod: float32 [2, 768, 4608], P(None, None, 'tensor'), may hold values from -0.21875 to 0.21875
- b_mod: float32 [2, 4608], P(None, 'tensor'), may hold values from -0.75 to 0.75
Outputs:
- outputs: float32 [16, 256, 768], P('dp')
- grad_inputs: float32 [16, 256, 768], P('dp')
- grad_condition: float32 [16, 768], P('dp')
- grad_w_qkv: float32 [2, 768, 3, 768], P(None, 'dp', None, 'tensor')
- grad_b_qv: float32 [2, 2, 768], P(None, None, 'tensor')
- grad_w_out: float32 [2, 768, 768], P(None, 'tensor', 'dp')
- grad_b_out: float32 [2, 768], replicated
- grad_w_up: float32 [2, 768, 3072], P(None, 'dp', 'tensor')
- grad_b_up: float32 [2, 3072], P(None, 'tensor')
- grad_w_down: float32 [2, 3072, 768], P(None, 'tensor', 'dp')
- grad_b_down: float32 [2, 768], replicated
- grad_w_mod: float32 [2, 768, 4608], P(None, 'dp', 'tensor')
- grad_b_mod: float32 [2, 4608], P(None, 'tensor')
All inputs are finite; a program needn't handle non-finite values.
Results may differ from a plain program's by a relative error of at most 0.0003.
Values sent between devices are 32-bit elements; how exact they have to be, the bound alone decides.
A program may use at most 256 MiB of HBM per device.

v0:
```python
import jax
import jax.numpy as jnp
from jax import lax
from jax.sharding import PartitionSpec as P

HEAD_DIM = 64


highest = lax.Precision.HIGHEST
eps_norm = 1e-06


def layer_norm(values):
    row_mean = jnp.mean(values, axis=-1, keepdims=True)
    centred = values - row_mean
    row_var = jnp.mean(centred * centred, axis=-1, keepdims=True)
    return centred * lax.rsqrt(row_var + eps_norm)


def gelu_tanh(values):
    return jax.nn.gelu(values, approximate=True)


def silu_slope(values):
    sigma = jax.nn.sigmoid(values)
    return sigma * (1.0 + values * (1.0 - sigma))


def join_branch(resid, gate, partial_value, bias):
    branch = lax.psum(partial_value, "tensor") + bias
    return (resid + gate[:, None, :] * branch, branch)


def gate_grad(grad, branch):
    return jnp.sum(grad * branch, axis=1)


def input_grad(partial_value):
    return lax.psum(partial_value, "tensor")


def on_device(
    inputs,
    condition,
    cotangent,
    w_qkv,
    b_qv,
    w_out,
    b_out,
    w_up,
    b_up,
    w_down,
    b_down,
    w_mod,
    b_mod,
):
    layers = w_qkv.shape[0]
    batch, seq_len, width = inputs.shape
    local_width = w_qkv.shape[3]
    heads_local = local_width // HEAD_DIM
    mod_cols = w_mod.shape[2]
    score_scale = HEAD_DIM ** (-0.5)
    activated = jax.nn.silu(condition)
    mod_local = jnp.einsum("bd,ldm->lbm", activated, w_mod, precision=highest) + b_mod[:, None, :]
    mod_whole = lax.all_gather(mod_local, "tensor", axis=2, tiled=True).reshape(
        layers, batch, 6, width
    )
    kept = []
    hidden = inputs
    for layer_index in range(layers):
        modulation = mod_whole[layer_index]
        shift_a, scale_a, gate_a = (modulation[:, 0], modulation[:, 1], modulation[:, 2])
        shift_b, scale_b, gate_b = (modulation[:, 3], modulation[:, 4], modulation[:, 5])
        modul_a = layer_norm(hidden) * (1.0 + scale_a[:, None, :]) + shift_a[:, None, :]
        projected = jnp.einsum("bsd,dcm->bscm", modul_a, w_qkv[layer_index], precision=highest)
        queries = (projected[:, :, 0] + b_qv[layer_index, 0]).reshape(
            batch, seq_len, heads_local, HEAD_DIM
        )
        keys = projected[:, :, 1].reshape(batch, seq_len, heads_local, HEAD_DIM)
        values = (projected[:, :, 2] + b_qv[layer_index, 1]).reshape(
            batch, seq_len, heads_local, HEAD_DIM
        )
        scores = jnp.einsum("bqhe,bkhe->bhqk", queries, keys, precision=highest) * score_scale
        log_norm = jax.nn.logsumexp(scores, axis=-1, keepdims=True)
        probs = jnp.exp(scores - log_norm)
        attended = jnp.einsum("bhqk,bkhe->bqhe", probs, values, precision=highest).reshape(
            batch, seq_len, local_width
        )
        partial_a = jnp.einsum("bsh,hd->bsd", attended, w_out[layer_index], precision=highest)
        middle, attn_branch = join_branch(hidden, gate_a, partial_a, b_out[layer_index])
        modul_b = layer_norm(middle) * (1.0 + scale_b[:, None, :]) + shift_b[:, None, :]
        pre_act = (
            jnp.einsum("bsd,df->bsf", modul_b, w_up[layer_index], precision=highest)
            + b_up[layer_index]
        )
        activ = gelu_tanh(pre_act)
        partial_b = jnp.einsum("bsf,fd->bsd", activ, w_down[layer_index], precision=highest)
        result, mlp_branch = join_branch(middle, gate_b, partial_b, b_down[layer_index])
        kept.append(
            (
                hidden,
                modul_a,
                queries,
                keys,
                values,
                log_norm,
                attended,
                attn_branch,
                middle,
                modul_b,
                pre_act,
                activ,
                mlp_branch,
            )
        )
        hidden = result
    grad_hidden = cotangent
    silu_grad_part = jnp.zeros((batch, width), jnp.float32)
    matrix_grads = [None] * layers
    bias_grads = [None] * layers
    for layer_index in reversed(range(layers)):
        (
            layer_in,
            modul_a,
            queries,
            keys,
            values,
            log_norm,
            attended,
            attn_branch,
            middle,
            modul_b,
            pre_act,
            activ,
            mlp_branch,
        ) = kept[layer_index]
        modulation = mod_whole[layer_index]
        scale_a, gate_a = (modulation[:, 1], modulation[:, 2])
        scale_b, gate_b = (modulation[:, 4], modulation[:, 5])
        d_branch_b = grad_hidden * gate_b[:, None, :]
        d_gate_b = gate_grad(grad_hidden, mlp_branch)
        g_b_down = jnp.sum(d_branch_b, axis=(0, 1))
        g_w_down = jnp.einsum("bsf,bsd->fd", activ, d_branch_b, precision=highest)
        d_activ = jnp.einsum("bsd,fd->bsf", d_branch_b, w_down[layer_index], precision=highest)
        d_pre = jax.vjp(gelu_tanh, pre_act)[1](d_activ)[0]
        g_b_up = jnp.sum(d_pre, axis=(0, 1))
        g_w_up = jnp.einsum("bsd,bsf->df", modul_b, d_pre, precision=highest)
        d_modul_b = input_grad(
            jnp.einsum("bsf,df->bsd", d_pre, w_up[layer_index], precision=highest)
        )
        normed_b, norm_back_b = jax.vjp(layer_norm, middle)
        d_scale_b = jnp.sum(d_modul_b * normed_b, axis=1)
        d_shift_b = jnp.sum(d_modul_b, axis=1)
        d_middle = grad_hidden + norm_back_b(d_modul_b * (1.0 + scale_b[:, None, :]))[0]
        d_branch_a = d_middle * gate_a[:, None, :]
        d_gate_a = gate_grad(d_middle, attn_branch)
        g_b_out = jnp.sum(d_branch_a, axis=(0, 1))
        g_w_out = jnp.einsum("bsh,bsd->hd", attended, d_branch_a, precision=highest)
        d_attended = jnp.einsum(
            "bsd,hd->bsh", d_branch_a, w_out[layer_index], precision=highest
        ).reshape(batch, seq_len, heads_local, HEAD_DIM)
        scores = jnp.einsum("bqhe,bkhe->bhqk", queries, keys, precision=highest) * score_scale
        probs = jnp.exp(scores - log_norm)
        d_values = jnp.einsum("bhqk,bqhe->bkhe", probs, d_attended, precision=highest)
        d_probs = jnp.einsum("bqhe,bkhe->bhqk", d_attended, values, precision=highest)
        attended_heads = attended.reshape(batch, seq_len, heads_local, HEAD_DIM)
        row_dot = jnp.einsum("bqhe,bqhe->bhq", d_attended, attended_heads)[..., None]
        d_scores = probs * (d_probs - row_dot) * score_scale
        d_queries = jnp.einsum("bhqk,bkhe->bqhe", d_scores, keys, precision=highest)
        d_keys = jnp.einsum("bhqk,bqhe->bkhe", d_scores, queries, precision=highest)
        d_proj = jnp.stack([d_queries, d_keys, d_values], axis=2).reshape(
            batch, seq_len, 3, local_width
        )
        g_b_qv = jnp.stack(
            [jnp.sum(d_proj[:, :, 0], axis=(0, 1)), jnp.sum(d_proj[:, :, 2], axis=(0, 1))], axis=0
        )
        g_w_qkv = jnp.einsum("bsd,bscm->dcm", modul_a, d_proj, precision=highest)
        d_modul_a = input_grad(
            jnp.einsum("bscm,dcm->bsd", d_proj, w_qkv[layer_index], precision=highest)
        )
        normed_a, norm_back_a = jax.vjp(layer_norm, layer_in)
        d_scale_a = jnp.sum(d_modul_a * normed_a, axis=1)
        d_shift_a = jnp.sum(d_modul_a, axis=1)
        grad_hidden = d_middle + norm_back_a(d_modul_a * (1.0 + scale_a[:, None, :]))[0]
        d_mod = jnp.stack(
            [d_shift_a, d_scale_a, d_gate_a, d_shift_b, d_scale_b, d_gate_b], axis=1
        ).reshape(batch, 6 * width)
        own_cols = lax.dynamic_slice_in_dim(d_mod, lax.axis_index("tensor") * mod_cols, mod_cols, 1)
        g_w_mod = jnp.einsum("bd,bm->dm", activated, own_cols, precision=highest)
        g_b_mod = jnp.sum(own_cols, axis=0)
        silu_grad_part = silu_grad_part + jnp.einsum(
            "bm,dm->bd", own_cols, w_mod[layer_index], precision=highest
        )
        layer_mats = (g_w_qkv, g_w_out, g_w_up, g_w_down, g_w_mod)
        matrix_grads[layer_index] = layer_mats
        bias_grads[layer_index] = (g_b_qv, g_b_out, g_b_up, g_b_down, g_b_mod)
    stacked_mats = tuple(
        (
            jnp.stack([matrix_grads[index][member] for index in range(layers)], axis=0)
            for member in range(5)
        )
    )
    reduced_mats = (
        lax.psum_scatter(stacked_mats[0], "dp", scatter_dimension=1, tiled=True),
        lax.psum_scatter(stacked_mats[1], "dp", scatter_dimension=2, tiled=True),
        lax.psum_scatter(stacked_mats[2], "dp", scatter_dimension=1, tiled=True),
        lax.psum_scatter(stacked_mats[3], "dp", scatter_dimension=2, tiled=True),
        lax.psum_scatter(stacked_mats[4], "dp", scatter_dimension=1, tiled=True),
    )
    stacked_bias = tuple(
        (
            jnp.stack([bias_grads[index][member] for index in range(layers)], axis=0)
            for member in range(5)
        )
    )
    reduced_bias = lax.psum(stacked_bias, "dp")
    grad_condition = lax.psum(silu_grad_part, "tensor") * silu_slope(condition)
    return (
        hidden,
        grad_hidden,
        grad_condition,
        reduced_mats[0],
        reduced_bias[0],
        reduced_mats[1],
        reduced_bias[1],
        reduced_mats[2],
        reduced_bias[2],
        reduced_mats[3],
        reduced_bias[3],
        reduced_mats[4],
        reduced_bias[4],
    )


def solution(mesh):
    in_specs = (
        P("dp", None, None),
        P("dp", None),
        P("dp", None, None),
        P(None, None, None, "tensor"),
        P(None, None, "tensor"),
        P(None, "tensor", None),
        P(),
        P(None, None, "tensor"),
        P(None, "tensor"),
        P(None, "tensor", None),
        P(),
        P(None, None, "tensor"),
        P(None, "tensor"),
    )
    out_specs = (
        P("dp", None, None),
        P("dp", None, None),
        P("dp", None),
        P(None, "dp", None, "tensor"),
        P(None, None, "tensor"),
        P(None, "tensor", "dp"),
        P(),
        P(None, "dp", "tensor"),
        P(None, "tensor"),
        P(None, "tensor", "dp"),
        P(),
        P(None, "dp", "tensor"),
        P(None, "tensor"),
    )
    return jax.shard_map(
        on_device, mesh=mesh, in_specs=in_specs, out_specs=out_specs, check_vma=False
    )
```

profile of v0, /device:TPU:0, one launch (start us, length us, event | category | flops | bytes accessed | tf_op | source)
XLA Modules:
  0.0 1023.0 jit_solution(14621295652847340553)
XLA Ops:
  11.9 9.4 fusion.204
  21.3 5.4 all-gather
  28.0 5.5 fusion.64
  38.5 2.3 convolution_bitcast_fusion.9
  42.4 34.8 %all-reduce.14.cloned.1.call-done = f32[1,256,768]{2,1,0:T(8,128)} async-done(((f32[1,256,768]{2,1,0:T(8,128)}), f32[1,256,768]{2,1,0:T(8,128)}) %all-reduce.14.cloned.1.call-update) | async-done | bytes 786448 | tf_op jit(solution)/shard_map/psum | solution.py:30
  79.3 6.2 fusion.42
  86.7 7.8 fusion.79
  97.6 31.4 %all-reduce.16.cloned.1.call-done = f32[1,256,768]{2,1,0:T(8,128)} async-done(((f32[1,256,768]{2,1,0:T(8,128)}), f32[1,256,768]{2,1,0:T(8,128)}) %all-reduce.16.cloned.1.call-update) | async-done | bytes 786448 | tf_op jit(solution)/shard_map/psum | solution.py:30
  131.2 5.5 fusion.67
  141.4 2.8 fusion.246
  146.4 2.3 convolution_bitcast_fusion.8
  149.0 34.2 %all-reduce.18.cloned.1.call-done = f32[1,256,768]{2,1,0:T(8,128)} async-done(((f32[1,256,768]{2,1,0:T(8,128)}), f32[1,256,768]{2,1,0:T(8,128)}) %all-reduce.18.cloned.1.call-update) | async-done | bytes 786448 | tf_op jit(solution)/shard_map/psum | solution.py:30
  185.2 6.4 fusion.45
  191.7 8.1 fusion.247
  201.0 5.1 fusion.82
  206.4 3.2 fusion.242
  209.6 31.0 %all-reduce.20.cloned.1.call-done = f32[1,256,768]{2,1,0:T(8,128)} async-done(((f32[1,256,768]{2,1,0:T(8,128)}), f32[1,256,768]{2,1,0:T(8,128)}) %all-reduce.20.cloned.1.call-update) | async-done | bytes 786448 | tf_op jit(solution)/shard_map/psum | solution.py:39
  240.6 2.4 multiply_reduce_fusion.5
  247.0 3.0 bitcast_reduce_fusion
  258.4 6.5 fusion.73
  265.4 34.0 %all-reduce.22.cloned.1.call-done = f32[1,256,768]{2,1,0:T(8,128)} async-done(((f32[1,256,768]{2,1,0:T(8,128)}), f32[1,256,768]{2,1,0:T(8,128)}) %all-reduce.22.cloned.1.call-update) | async-done | bytes 786448 | tf_op jit(solution)/shard_map/psum | solution.py:39
  304.7 7.5 fusion.248
  313.4 7.4 fusion.76
  321.1 8.2 fusion.85
  329.3 26.0 %all-reduce.24.cloned.1.call-done = f32[1,256,768]{2,1,0:T(8,128)} async-done(((f32[1,256,768]{2,1,0:T(8,128)}), f32[1,256,768]{2,1,0:T(8,128)}) %all-reduce.24.cloned.1.call-update) | async-done | bytes 786448 | tf_op jit(solution)/shard_map/psum | solution.py:39
  361.3 3.0 bitcast_reduce_fusion.2
  370.1 6.7 fusion.70
  377.4 6.3 convolution_bitcast_fusion
  386.1 4.8 convolution_bitcast_fusion.1
  390.8 4.2 pad_maximum_fusion.2
  395.1 15.5 %copy.105 = f32[2,1536,768]{1,0,2:T(2,128)} copy(f32[2,1536,768]{2,1,0:T(8,128)} %pad_maximum_fusion.2) | data formatting | bytes 18874368 | tf_op jit(solution)/shard_map/stack | solution.py:199
  413.4 5.3 copy.104
  420.0 4.6 convolution_bitcast_fusion.4
  424.7 3.8 convolution_bitcast_fusion.5
  428.4 3.3 pad_maximum_fusion.3
  432.9 5.8 convolution_bitcast_fusion.2
  438.8 4.4 convolution_bitcast_fusion.3
  443.2 4.4 pad_maximum_fusion.1
  451.8 6.1 multiply_bitcast_fusion.1
  457.9 11.1 %pad_maximum_fusion = f32[2,768,2304]{2,1,0:T(8,128)} fusion(f32[1,768,2304]{2,1,0:T(8,128)} %get-tuple-element.138, f32[1,768,2304]{2,1,0:T(8,128)} %get-tuple-element.137), kind=kLoop, calls=%fused_computation | loop fusion | flops 3538944 | bytes 28311552 | tf_op jit(solution)/shard_map/stack | solution.py:199
  471.4 7.9 fusion.97
  479.4 7.9 fusion.94
  487.3 5.1 psum.106
  492.5 62.9 %all-reduce.2 = (f32[2,2,384]{2,1,0:T(2,128)}, f32[2,768]{1,0:T(2,128)}, f32[2,1536]{1,0:T(2,128)}, f32[2,768]{1,0:T(2,128)}, f32[2,2304]{1,0:T(2,128)}) all-reduce(f32[2,2,384]{2,1,0:T(2,128)S(1)} %pad_maximum_fusion.7, f32[2,768]{1,0:T(2,128)S(1)} %get-tuple-element.163, ...), channel_id=1, replica_groups=mesh['dp'=16,'tensor'=2] {'dp'}, use_global_device_ids=true, to_apply=%region_46.47 | all-reduce | flops 12288 | bytes 98304 | tf_op jit(solution)/shard_map/psum | solution.py:216
  557.3 97.5 %all-reduce.26.cloned.1.call-done = (f32[2,384,768]{1,0,2:T(2,128)}, f32[2,1536,768]{1,0,2:T(2,128)}) async-done(((f32[2,384,768]{1,0,2:T(2,128)}, f32[2,1536,768]{1,0,2:T(2,128)}), (f32[2,384,768]{1,0,2:T(2,128)}, f32[2,1536,768]{1,0,2:T(2,128)})) %all-reduce.26.cloned.1.call-update) | async-done | bytes 11796496
  658.5 91.7 %reduce-scatter.4.cloned.1.call-done = f32[2,48,3,384]{3,1,2,0:T(8,128)} async-done(((f32[2,768,3,384]{3,1,2,0:T(8,128)}), f32[2,48,3,384]{3,1,2,0:T(8,128)}) %reduce-scatter.4.cloned.1.call-update) | async-done | bytes 442384 | tf_op jit(solution)/shard_map/reduce_scatter | solution.py:204
  750.2 115.4 %reduce-scatter.6.cloned.1.call-done = f32[2,48,1536]{2,1,0:T(8,128)} async-done(((f32[2,768,1536]{2,1,0:T(8,128)}), f32[2,48,1536]{2,1,0:T(8,128)}) %reduce-scatter.6.cloned.1.call-update) | async-done | bytes 589840 | tf_op jit(solution)/shard_map/reduce_scatter | solution.py:206
  865.6 150.7 %reduce-scatter.8.cloned.1.call-done = f32[2,48,2304]{2,1,0:T(8,128)} async-done(((f32[2,768,2304]{2,1,0:T(8,128)}), f32[2,48,2304]{2,1,0:T(8,128)}) %reduce-scatter.8.cloned.1.call-update) | async-done | bytes 884752 | tf_op jit(solution)/shard_map/reduce_scatter | solution.py:208
  (491 shorter events, 81.2 us)
Async XLA Ops:
  7.2 69.9 %all-reduce.14.cloned.1.call-start = ((), (), s32[]{:S(2)}) async-start(), calls=%async_computation.3 | async-start | bytes 1572864 | tf_op jit(solution)/shard_map/psum | solution.py:30
  8.5 19.5 %copy-start.102 = (f32[256]{0:T(256)}, f32[256]{0:T(256)S(1)}, u32[]{:S(2)}) copy-start(f32[256]{0:T(256)S(1)} %broadcast_multiply_fusion.3) | copy-start | bytes 3076
  9.9 18.1 %copy-start.120 = (f32[256]{0:T(256)}, f32[256]{0:T(256)S(1)}, u32[]{:S(2)}) copy-start(f32[256]{0:T(256)S(1)} %fusion.206) | copy-start | bytes 3076
  10.5 10.8 %copy-start.118 = (f32[1,768]{1,0:T(1,128)}, f32[1,768]{1,0:T(1,128)S(1)}, u32[]{:S(2)}) copy-start(f32[1,768]{1,0:T(1,128)S(1)} %get-tuple-element.108) | copy-start | bytes 9220
  11.2 23.7 %copy-start.85 = (f32[6,64]{1,0:T(8,128)}, f32[6,64]{1,0:T(8,128)S(1)}, u32[]{:S(2)}) copy-start(f32[6,64]{1,0:T(8,128)S(1)} %add.361) | copy-start | bytes 4612
  11.9 9.4 copy-start.130
  11.9 16.1 %copy-start = (f32[1,256,768]{2,1,0:T(8,128)S(1)}, f32[1,256,768]{2,1,0:T(8,128)}, u32[]{:S(2)}) copy-start(f32[1,256,768]{2,1,0:T(8,128)} %param.13) | copy-start | bytes 2359300
  28.0 49.2 %copy-start.70 = (f32[768]{0:T(1024)}, f32[768]{0:T(1024)S(1)}, u32[]{:S(2)}) copy-start(f32[768]{0:T(1024)S(1)} %get-tuple-element.85) | copy-start | bytes 9220
  28.0 50.8 %copy-start.68 = (f32[768]{0:T(1024)}, f32[768]{0:T(1024)S(1)}, u32[]{:S(2)}) copy-start(f32[768]{0:T(1024)S(1)} %get-tuple-element.82) | copy-start | bytes 9220
  40.9 88.2 %all-reduce.16.cloned.1.call-start = ((), (), s32[]{:S(2)}) async-start(), calls=%async_computation.4 | async-start | bytes 1572864 | tf_op jit(solution)/shard_map/psum | solution.py:30
  78.5 50.5 %copy-start.4 = (f32[1,256,768]{2,1,0:T(8,128)}, f32[1,256,768]{2,1,0:T(8,128)S(1)}, u32[]{:S(2)}) copy-start(f32[1,256,768]{2,1,0:T(8,128)S(1)} %get-tuple-element.127) | copy-start | bytes 2359300
  86.7 8.3 copy-start.161
  86.7 8.9 copy-start.160
  86.7 9.6 copy-start.80
  86.7 9.6 copy-start.166
  94.5 88.7 %all-reduce.18.cloned.1.call-start = ((), (), s32[]{:S(2)}) async-start(), calls=%async_computation.5 | async-start | bytes 1572864 | tf_op jit(solution)/shard_map/psum | solution.py:30
  97.0 33.7 %copy-start.82 = (f32[768]{0:T(1024)}, f32[768]{0:T(1024)S(1)}, u32[]{:S(2)}) copy-start(f32[768]{0:T(1024)S(1)} %get-tuple-element.89) | copy-start | bytes 9220
  97.6 33.1 %copy-start.75 = (f32[768]{0:T(1024)}, f32[768]{0:T(1024)S(1)}, u32[]{:S(2)}) copy-start(f32[768]{0:T(1024)S(1)} %get-tuple-element.78) | copy-start | bytes 9220
  148.8 91.8 %all-reduce.20.cloned.1.call-start = ((), (), s32[]{:S(2)}) async-start(), calls=%async_computation.6 | async-start | bytes 1572864 | tf_op jit(solution)/shard_map/psum | solution.py:39
  185.2 15.8 %slice-start = ((s8[9437184]{0:T(1024)(128)(4,1)}), s8[1048576]{0:T(1024)(128)(4,1)S(1)}, s32[]{:S(2)}) async-start(s8[9437184]{0:T(1024)(128)(4,1)} %bitcast.293), calls=%async_computation.14 | async-start | bytes 2097152
  185.2 15.8 %slice-start.1 = ((s8[9437184]{0:T(1024)(128)(4,1)}), s8[4194304]{0:T(1024)(128)(4,1)S(1)}, s32[]{:S(2)}) async-start(s8[9437184]{0:T(1024)(128)(4,1)} %bitcast.293), calls=%async_computation.15 | async-start | bytes 8388608
  191.7 8.1 copy-start.26
  191.7 9.3 slice-start.2
  206.1 93.3 %all-reduce.22.cloned.1.call-start = ((), (), s32[]{:S(2)}) async-start(), calls=%async_computation.7 | async-start | bytes 1572864 | tf_op jit(solution)/shard_map/psum | solution.py:39
  256.1 8.8 copy-start.40
  257.4 7.5 copy-start.42
  258.4 41.0 %copy-start.3 = (f32[1,256,768]{2,1,0:T(8,128)S(1)}, f32[1,256,768]{2,1,0:T(8,128)}, u32[]{:S(2)}) copy-start(f32[1,256,768]{2,1,0:T(8,128)} %copy-done.2) | copy-start | bytes 2359300
  258.4 41.0 %copy-start.76 = (f32[768]{0:T(1024)S(1)}, f32[768]{0:T(1024)}, u32[]{:S(2)}) copy-start(f32[768]{0:T(1024)} %copy-done.75) | copy-start | bytes 9220
  258.4 41.0 %copy-start.110 = (f32[256]{0:T(256)S(1)}, f32[256]{0:T(256)}, u32[]{:S(2)}) copy-start(f32[256]{0:T(256)} %copy-done.109) | copy-start | bytes 3076
  264.9 90.4 %all-reduce.24.cloned.1.call-start = ((), (), s32[]{:S(2)}) async-start(), calls=%async_computation.8 | async-start | bytes 1572864 | tf_op jit(solution)/shard_map/psum | solution.py:39
  304.2 8.0 copy-start.57
  320.8 34.5 %copy-start.5 = (f32[1,256,768]{2,1,0:T(8,128)S(1)}, f32[1,256,768]{2,1,0:T(8,128)}, u32[]{:S(2)}) copy-start(f32[1,256,768]{2,1,0:T(8,128)} %copy-done.4) | copy-start | bytes 2359300
  320.8 34.5 %copy-start.69 = (f32[768]{0:T(1024)S(1)}, f32[768]{0:T(1024)}, u32[]{:S(2)}) copy-start(f32[768]{0:T(1024)} %copy-done.68) | copy-start | bytes 9220
  320.9 34.5 %copy-start.106 = (f32[256]{0:T(256)S(1)}, f32[256]{0:T(256)}, u32[]{:S(2)}) copy-start(f32[256]{0:T(256)} %copy-done.105) | copy-start | bytes 3076
  320.9 127.6 %all-reduce.28.cloned.1.call-start = ((), (), s32[]{:S(2)}) async-start(), calls=%async_computation.13 | async-start | bytes 3145728 | tf_op jit(solution)/shard_map/psum | solution.py:30
  369.7 7.1 copy-start.45
  376.8 7.0 copy-start.14
  376.8 7.0 copy-start.22
  376.8 7.0 copy-start.79
  376.8 278.0 %all-reduce.26.cloned.1.call-start = ((), (), s32[]{:S(2)}) async-start(), calls=%async_computation.12 | async-start | bytes 23592960
  395.1 15.5 %copy-start.10 = (f32[1,256,768]{2,1,0:T(8,128)S(1)}, f32[1,256,768]{2,1,0:T(8,128)}, u32[]{:S(2)}) copy-start(f32[1,256,768]{2,1,0:T(8,128)} %copy-done.9) | copy-start | bytes 2359300
  418.8 331.3 %reduce-scatter.4.cloned.1.call-start = ((), (), s32[]{:S(2)}) async-start(), calls=%async_computation.9 | async-start | bytes 7520256 | tf_op jit(solution)/shard_map/reduce_scatter | solution.py:204
  431.8 433.7 %reduce-scatter.6.cloned.1.call-start = ((), (), s32[]{:S(2)}) async-start(), calls=%async_computation.10 | async-start | bytes 10027008 | tf_op jit(solution)/shard_map/reduce_scatter | solution.py:206
  447.7 568.5 %reduce-scatter.8.cloned.1.call-start = ((), (), s32[]{:S(2)}) async-start(), calls=%async_computation.11 | async-start | bytes 15040512 | tf_op jit(solution)/shard_map/reduce_scatter | solution.py:208
  479.4 76.0 %copy-start.154 = (f32[256]{0:T(256)S(1)}, f32[256]{0:T(256)}, u32[]{:S(2)}) copy-start(f32[256]{0:T(256)} %copy-done.153) | copy-start | bytes 3076
  487.3 68.4 %copy-start.117 = (f32[1,768]{1,0:T(1,128)S(1)}, f32[1,768]{1,0:T(1,128)}, u32[]{:S(2)}) copy-start(f32[1,768]{1,0:T(1,128)} %param.14) | copy-start | bytes 9220
  487.3 68.4 %copy-start.119 = (f32[1,768]{1,0:T(1,128)S(1)}, f32[1,768]{1,0:T(1,128)}, u32[]{:S(2)}) copy-start(f32[1,768]{1,0:T(1,128)} %copy-done.118) | copy-start | bytes 9220
  487.3 69.0 %copy-start.11 = (f32[1,256,768]{2,1,0:T(8,128)S(1)}, f32[1,256,768]{2,1,0:T(8,128)}, u32[]{:S(2)}) copy-start(f32[1,256,768]{2,1,0:T(8,128)} %copy-done.9) | copy-start | bytes 2359300
  (134 other events, 335.3 us)
Sparse Core Ops, SparseCore 0:
  41.0 36.1 all-reduce.13
  94.7 34.3 all-reduce.15
  148.9 34.2 all-reduce.17
  206.2 34.3 all-reduce.19
  265.1 34.2 all-reduce.21
  321.0 34.3 all-reduce.23
  376.9 51.6 all-reduce.27
  433.0 221.7 all-reduce.25
  659.9 90.1 reduce-scatter.3
  754.7 110.8 reduce-scatter.5
  870.9 145.3 reduce-scatter.7
where the time goes:
time: 1030 us; the launch traced here: 1020 us
  waiting for transfers between devices  647 us (63%)
  matrix products  170 us (17%)
  blocking collectives  73.3 us (7%)
  other arithmetic  56.9 us (6%)
  local copies, waits for them, and re-layouts  56.4 us (5%)
  between operations  16.8 us (2%)
    reduce_scatter x1, waiting for transfers between devices, on_device(): lax.psum_scatter(stacked_mats[4], 'dp', scatter_dimension=1, tiled=True)  151 us
    reduce_scatter x1, waiting for transfers between devices, on_device(): lax.psum_scatter(stacked_mats[2], 'dp', scatter_dimension=1, tiled=True)  115 us
    psum x4, waiting for transfers between devices, join_branch(): branch = lax.psum(partial_value, 'tensor') + bias  100 us
    unnamed x12, waiting for transfers between devices  97.7 us
    reduce_scatter x1, waiting for transfers between devices, on_device(): lax.psum_scatter(stacked_mats[0], 'dp', scatter_dimension=1, tiled=True)  91.7 us
    psum x3, waiting for transfers between devices, input_grad(): return lax.psum(partial_value, 'tensor')  91.1 us
    psum x1, blocking collectives, on_device(): reduced_bias = lax.psum(stacked_bias, 'dp')  62.9 us
    another operation x6, other arithmetic, on_device(): jnp.stack([matrix_grads[index][member] for index in range(layers)], axis=0)  30.7 us
  transfers between devices with their start and end apart: 11, of which 10 were waited for; matrix products, arithmetic and copies ran while one was open for 12% of the time, Pallas kernels for 0%

commit v1 on v0

v1 whole, which is shorter than its diff:
```python
import jax
import jax.numpy as jnp
from jax import lax
from jax.sharding import PartitionSpec as P

HEAD_DIM = 64


high = lax.Precision.HIGH
eps_norm = 1e-06


def layer_norm(values):
    row_mean = jnp.mean(values, axis=-1, keepdims=True)
    centred = values - row_mean
    row_var = jnp.mean(centred * centred, axis=-1, keepdims=True)
    return centred * lax.rsqrt(row_var + eps_norm)


def gelu_tanh(values):
    return jax.nn.gelu(values, approximate=True)


def silu_slope(values):
    sigma = jax.nn.sigmoid(values)
    return sigma * (1.0 + values * (1.0 - sigma))


def pair_sum(value):
    if lax.axis_size("tensor") == 2:
        return value + lax.ppermute(value, "tensor", [(0, 1), (1, 0)])
    return lax.psum(value, "tensor")


def pair_gather(value, axis):
    if lax.axis_size("tensor") == 2:
        other = lax.ppermute(value, "tensor", [(0, 1), (1, 0)])
        first = lax.axis_index("tensor") == 0
        low = jnp.where(first, value, other)
        top = jnp.where(first, other, value)
        return jnp.concatenate([low, top], axis=axis)
    return lax.all_gather(value, "tensor", axis=axis, tiled=True)


def vec_mat(vec, mat):
    if vec.shape[0] == 1:
        return jnp.sum(vec[0][:, None] * mat, axis=0)[None]
    return jnp.einsum("bk,km->bm", vec, mat, precision=high)


def vec_mat_t(vec, mat):
    if vec.shape[0] == 1:
        return jnp.sum(vec[0][None, :] * mat, axis=1)[None]
    return jnp.einsum("bm,km->bk", vec, mat, precision=high)


def scattered_grad(left, right):
    tokens = left.shape[0] * left.shape[1]
    rows = left.shape[2]
    cols = right.shape[2]
    left_t = left.reshape(tokens, rows).T
    right = right.reshape(tokens, cols)
    count = lax.axis_size("dp")
    if count & (count - 1) or count < 2:
        whole = jnp.dot(left_t, right, precision=high)
        return lax.psum_scatter(whole, "dp", scatter_dimension=0, tiled=True)
    block = rows // count
    index = lax.axis_index("dp")
    bit = index % 2
    blocks = left_t.reshape(count // 2, 2, block, tokens)

    def product(which):
        chosen = lax.dynamic_index_in_dim(blocks, which, 1, keepdims=False)
        return jnp.dot(chosen.reshape(rows // 2, tokens), right, precision=high)

    pairs = [(device, device ^ 1) for device in range(count)]
    arrived = lax.ppermute(product(1 - bit), "dp", pairs)
    total = product(bit) + arrived
    step = 2
    groups = count // 2
    while groups > 1:
        bit = (index // step) % 2
        parts = total.reshape(groups // 2, 2, block, cols)
        away = lax.dynamic_index_in_dim(parts, 1 - bit, 1, keepdims=False)
        kept = lax.dynamic_index_in_dim(parts, bit, 1, keepdims=False)
        pairs = [(device, device ^ step) for device in range(count)]
        total = kept + lax.ppermute(away, "dp", pairs)
        groups //= 2
        step *= 2
    return total.reshape(block, cols)

def on_device(
    inputs,
    condition,
    cotangent,
    w_qkv,
    b_qv,
    w_out,
    b_out,
    w_up,
    b_up,
    w_down,
    b_down,
    w_mod,
    b_mod,
):
    layers = w_qkv.shape[0]
    batch, seq_len, width = inputs.shape
    local_width = w_qkv.shape[3]
    heads_local = local_width // HEAD_DIM
    mod_cols = w_mod.shape[2]
    score_scale = HEAD_DIM ** (-0.5)
    activated = jax.nn.silu(condition)
    mod_local = (
        jnp.stack([vec_mat(activated, w_mod[index]) for index in range(layers)], axis=0)
        + b_mod[:, None, :]
    )
    mod_whole = pair_gather(mod_local, 2).reshape(layers, batch, 6, width)
    activated_all = lax.all_gather(activated, "dp", axis=0, tiled=True)
    kept = []
    hidden = inputs
    for layer_index in range(layers):
        modulation = mod_whole[layer_index]
        shift_a, scale_a, gate_a = (modulation[:, 0], modulation[:, 1], modulation[:, 2])
        shift_b, scale_b, gate_b = (modulation[:, 3], modulation[:, 4], modulation[:, 5])
        modul_a = layer_norm(hidden) * (1.0 + scale_a[:, None, :]) + shift_a[:, None, :]
        projected = jnp.einsum("bsd,dcm->bscm", modul_a, w_qkv[layer_index], precision=high)
        queries = (projected[:, :, 0] + b_qv[layer_index, 0]).reshape(
            batch, seq_len, heads_local, HEAD_DIM
        )
        keys = projected[:, :, 1].reshape(batch, seq_len, heads_local, HEAD_DIM)
        values = (projected[:, :, 2] + b_qv[layer_index, 1]).reshape(
            batch, seq_len, heads_local, HEAD_DIM
        )
        scores = jnp.einsum("bqhe,bkhe->bhqk", queries, keys, precision=high) * score_scale
        log_norm = jax.nn.logsumexp(scores, axis=-1, keepdims=True)
        probs = jnp.exp(scores - log_norm)
        attended = jnp.einsum("bhqk,bkhe->bqhe", probs, values, precision=high).reshape(
            batch, seq_len, local_width
        )
        partial_a = jnp.einsum("bsh,hd->bsd", attended, w_out[layer_index], precision=high)
        attn_branch = pair_sum(partial_a) + b_out[layer_index]
        middle = hidden + gate_a[:, None, :] * attn_branch
        modul_b = layer_norm(middle) * (1.0 + scale_b[:, None, :]) + shift_b[:, None, :]
        pre_act = (
            jnp.einsum("bsd,df->bsf", modul_b, w_up[layer_index], precision=high)
            + b_up[layer_index]
        )
        activ = gelu_tanh(pre_act)
        partial_b = jnp.einsum("bsf,fd->bsd", activ, w_down[layer_index], precision=high)
        mlp_branch = pair_sum(partial_b) + b_down[layer_index]
        result = middle + gate_b[:, None, :] * mlp_branch
        kept.append(
            (
                hidden,
                modul_a,
                queries,
                keys,
                values,
                probs,
                attended,
                attn_branch,
                middle,
                modul_b,
                pre_act,
                activ,
                mlp_branch,
            )
        )
        hidden = result
    grad_hidden = cotangent
    silu_grad_part = jnp.zeros((batch, width), jnp.float32)
    matrix_grads = [None] * layers
    pieces = [None] * layers
    for layer_index in reversed(range(layers)):
        (
            layer_in,
            modul_a,
            queries,
            keys,
            values,
            probs,
            attended,
            attn_branch,
            middle,
            modul_b,
            pre_act,
            activ,
            mlp_branch,
        ) = kept[layer_index]
        modulation = mod_whole[layer_index]
        scale_a, gate_a = (modulation[:, 1], modulation[:, 2])
        scale_b, gate_b = (modulation[:, 4], modulation[:, 5])
        d_branch_b = grad_hidden * gate_b[:, None, :]
        d_gate_b = jnp.sum(grad_hidden * mlp_branch, axis=1)
        g_b_down = jnp.sum(d_branch_b, axis=(0, 1))
        g_w_down = scattered_grad(d_branch_b, activ)
        d_activ = jnp.einsum("bsd,fd->bsf", d_branch_b, w_down[layer_index], precision=high)
        d_pre = jax.vjp(gelu_tanh, pre_act)[1](d_activ)[0]
        g_b_up = jnp.sum(d_pre, axis=(0, 1))
        g_w_up = scattered_grad(modul_b, d_pre)
        d_modul_b = pair_sum(
            jnp.einsum("bsf,df->bsd", d_pre, w_up[layer_index], precision=high)
        )
        normed_b, norm_back_b = jax.vjp(layer_norm, middle)
        d_scale_b = jnp.sum(d_modul_b * normed_b, axis=1)
        d_shift_b = jnp.sum(d_modul_b, axis=1)
        d_middle = grad_hidden + norm_back_b(d_modul_b * (1.0 + scale_b[:, None, :]))[0]
        d_branch_a = d_middle * gate_a[:, None, :]
        d_gate_a = jnp.sum(d_middle * attn_branch, axis=1)
        g_b_out = jnp.sum(d_branch_a, axis=(0, 1))
        g_w_out = scattered_grad(d_branch_a, attended)
        d_attended = jnp.einsum(
            "bsd,hd->bsh", d_branch_a, w_out[layer_index], precision=high
        ).reshape(batch, seq_len, heads_local, HEAD_DIM)
        d_values = jnp.einsum("bhqk,bqhe->bkhe", probs, d_attended, precision=high)
        d_probs = jnp.einsum("bqhe,bkhe->bhqk", d_attended, values, precision=high)
        attended_heads = attended.reshape(batch, seq_len, heads_local, HEAD_DIM)
        row_dot = jnp.transpose(jnp.sum(d_attended * attended_heads, axis=-1), (0, 2, 1))[..., None]
        d_scores = probs * (d_probs - row_dot) * score_scale
        d_queries = jnp.einsum("bhqk,bkhe->bqhe", d_scores, keys, precision=high)
        d_keys = jnp.einsum("bhqk,bqhe->bkhe", d_scores, queries, precision=high)
        d_proj = jnp.stack([d_queries, d_keys, d_values], axis=2).reshape(
            batch, seq_len, 3, local_width
        )
        d_flat = d_proj.reshape(batch, seq_len, 3 * local_width)
        g_b_qv = jnp.sum(d_flat, axis=(0, 1))
        g_w_qkv = scattered_grad(modul_a, d_flat)
        d_modul_a = pair_sum(
            jnp.einsum("bscm,dcm->bsd", d_proj, w_qkv[layer_index], precision=high)
        )
        normed_a, norm_back_a = jax.vjp(layer_norm, layer_in)
        d_scale_a = jnp.sum(d_modul_a * normed_a, axis=1)
        d_shift_a = jnp.sum(d_modul_a, axis=1)
        grad_hidden = d_middle + norm_back_a(d_modul_a * (1.0 + scale_a[:, None, :]))[0]
        d_mod = jnp.stack(
            [d_shift_a, d_scale_a, d_gate_a, d_shift_b, d_scale_b, d_gate_b], axis=1
        ).reshape(batch, 6 * width)
        own_cols = lax.dynamic_slice_in_dim(d_mod, lax.axis_index("tensor") * mod_cols, mod_cols, 1)
        silu_grad_part = silu_grad_part + vec_mat_t(own_cols, w_mod[layer_index])
        matrix_grads[layer_index] = (g_w_qkv, g_w_out, g_w_up, g_w_down)
        pieces[layer_index] = (own_cols, (g_b_qv, g_b_out, g_b_up, g_b_down))
    block = width // lax.axis_size("dp")
    activated_rows = lax.dynamic_slice_in_dim(
        activated_all, lax.axis_index("dp") * block, block, 1
    )
    mod_grads = [None] * layers
    bias_grads = [None] * layers
    for layer_index in reversed(range(layers)):
        own_cols, biases = pieces[layer_index]
        line = jnp.concatenate(biases)[None]
        line = jnp.concatenate([line, jnp.zeros((batch - 1, line.shape[1]), line.dtype)], axis=0)
        gathered = lax.all_gather(
            jnp.concatenate([own_cols, line], axis=1), "dp", axis=0, tiled=True
        )
        mod_grads[layer_index] = jnp.einsum(
            "bd,bm->dm", activated_rows, gathered[:, :mod_cols], precision=high
        )
        sums = jnp.sum(gathered, axis=0)
        found = [sums[:mod_cols]]
        start = mod_cols
        for piece in biases:
            found.append(sums[start : start + piece.shape[0]])
            start += piece.shape[0]
        bias_grads[layer_index] = found
    order = range(layers)
    grad_w_qkv = jnp.stack([matrix_grads[index][0] for index in order], axis=0)
    grad_w_out = jnp.stack([matrix_grads[index][1].T for index in order], axis=0)
    grad_w_up = jnp.stack([matrix_grads[index][2] for index in order], axis=0)
    grad_w_down = jnp.stack([matrix_grads[index][3].T for index in order], axis=0)
    grad_b_mod, grad_b_qkv, grad_b_out, grad_b_up, grad_b_down = [
        jnp.stack([bias_grads[index][member] for index in order], axis=0) for member in range(5)
    ]
    grad_b_qv = grad_b_qkv.reshape(layers, 3, local_width)[:, ::2]
    grad_condition = pair_sum(silu_grad_part) * silu_slope(condition)
    return (
        hidden,
        grad_hidden,
        grad_condition,
        grad_w_qkv.reshape(layers, block, 3, local_width),
        grad_b_qv,
        grad_w_out,
        grad_b_out,
        grad_w_up,
        grad_b_up,
        grad_w_down,
        grad_b_down,
        jnp.stack(mod_grads, axis=0),
        grad_b_mod,
    )


def solution(mesh):
    in_specs = (
        P("dp", None, None),
        P("dp", None),
        P("dp", None, None),
        P(None, None, None, "tensor"),
        P(None, None, "tensor"),
        P(None, "tensor", None),
        P(),
        P(None, None, "tensor"),
        P(None, "tensor"),
        P(None, "tensor", None),
        P(),
        P(None, None, "tensor"),
        P(None, "tensor"),
    )
    out_specs = (
        P("dp", None, None),
        P("dp", None, None),
        P("dp", None),
        P(None, "dp", None, "tensor"),
        P(None, None, "tensor"),
        P(None, "tensor", "dp"),
        P(),
        P(None, "dp", "tensor"),
        P(None, "tensor"),
        P(None, "tensor", "dp"),
        P(),
        P(None, "dp", "tensor"),
        P(None, "tensor"),
    )
    return jax.shard_map(
        on_device, mesh=mesh, in_specs=in_specs, out_specs=out_specs, check_vma=False
    )
```

time: 1030 us -> 585 us (0.57)
  waiting for transfers between devices: 647 us -> 222 us
  matrix products: 170 us -> 126 us
  starting transfers between devices: 2.42 us -> 33 us
  between operations: 16.8 us -> 3.61 us
  local copies, waits for them, and re-layouts: 56.4 us -> 68.9 us
  blocking collectives: 73.3 us -> 62.3 us
    reduce_scatter x3 -> x0, waiting for transfers between devices: 358 us -> none  [the longest x1 151 us: on_device(): lax.psum_scatter(stacked_mats[4], 'dp', scatter_dimension=1, tiled=True)]
    ppermute x0 -> x42, waiting for transfers between devices: none -> 222 us  [the longest x24 163 us: scattered_grad(): total = kept + lax.ppermute(away, 'dp', pairs)]
    psum x7 -> x0, waiting for transfers between devices: 192 us -> none  [the longest x4 100 us: join_branch(): branch = lax.psum(partial_value, 'tensor') + bias]
    unnamed x12 -> x0, waiting for transfers between devices: 97.7 us -> none
    psum x2 -> x0, blocking collectives: 68 us -> none  [the longest x1 62.9 us: on_device(): reduced_bias = lax.psum(stacked_bias, 'dp')]
    all_gather x1 -> x3, blocking collectives: 5.36 us -> 62.3 us  [the longest x2 40.3 us: on_device(): lax.all_gather(jnp.concatenate([own_cols, line], axis=1), 'dp', axis=0, t...]
    dot_general x39 -> x46, matrix products: 170 us -> 126 us  [the longest x16 35.7 us: product(): return jnp.dot(chosen.reshape(rows // 2, tokens), right, precision=high)]
    ppermute x0 -> x42, starting transfers between devices: none -> 33 us  [the longest x24 18.2 us: scattered_grad(): total = kept + lax.ppermute(away, 'dp', pairs)]
  transfers between devices with their start and end apart: 11 -> 42, of which waited for: 10 -> 19; matrix products, arithmetic and copies ran while one was open for 12% -> 27% of each run, Pallas kernels for 0% -> 0%
where the time goes in v1:
time: 585 us; the launch traced here: 575 us
  waiting for transfers between devices  222 us (38%)
  matrix products  126 us (22%)
  local copies, waits for them, and re-layouts  68.9 us (12%)
  blocking collectives  62.3 us (11%)
  other arithmetic  58.5 us (10%)
  starting transfers between devices  33 us (6%)
    ppermute x24, waiting for transfers between devices, scattered_grad(): total = kept + lax.ppermute(away, 'dp', pairs)  163 us
    ppermute x9, waiting for transfers between devices, pair_sum(): return value + lax.ppermute(value, 'tensor', [(0, 1), (1, 0)])  59.2 us
    all_gather x2, blocking collectives, on_device(): lax.all_gather(jnp.concatenate([own_cols, line], axis=1), 'dp', axis=0, t...  40.3 us
    dot_general x16, matrix products, product(): return jnp.dot(chosen.reshape(rows // 2, tokens), right, precision=high)  35.7 us
    all_gather x1, blocking collectives, on_device(): activated_all = lax.all_gather(activated, 'dp', axis=0, tiled=True)  21.9 us
    dot_general x2, matrix products, on_device(): jnp.einsum('bsd,dcm->bscm', modul_a, w_qkv[layer_index], precision=high)  19.6 us
    ppermute x24, starting transfers between devices, scattered_grad(): total = kept + lax.ppermute(away, 'dp', pairs)  18.2 us
    transpose x8, local copies, waits for them, and re-layouts, scattered_grad(): left_t = left.reshape(tokens, rows).T  15.7 us
  transfers between devices with their start and end apart: 42, of which 19 were waited for; matrix products, arithmetic and copies ran while one was open for 27% of the time, Pallas kernels for 0%

profile of v1, /device:TPU:0, one launch (start us, length us, event | category | flops | bytes accessed | tf_op | source)
XLA Modules:
  0.0 574.5 jit_solution(8802800314265596121)
XLA Ops:
  2.7 5.8 %fusion.2 = (f32[2304]{0:T(1024)S(1)}, f32[2304]{0:T(1024)S(1)}) fusion(f32[2,768,2304]{2,1,0:T(8,128)} %param.24, f32[768]{0:T(1024)S(1)} %multiply_reduce_fusion.20), kind=kLoop, calls=%fused_computation.6 | loop fusion | flops 7073280 | bytes 14177280 | tf_op jit(solution)/shard_map/reduce_sum | solution.py:47
  8.6 3.0 collective-permute-start
  14.8 4.0 fusion.62
  26.7 15.8 %collective-permute-done.1 = f32[1,256,768]{2,1,0:T(8,128)S(1)} collective-permute-done((f32[1,256,768]{2,1,0:T(8,128)S(1)}, f32[1,256,768]{2,1,0:T(8,128)S(1)}, u32[]{:S(2)}, u32[]{:S(2)}) %collective-permute-start.1) | collective-permute-done | bytes 786464 | tf_op jit(solution)/shard_map/ppermute | solution.py:31
  44.2 4.7 fusion.40
  48.9 5.5 fusion.77
  59.7 13.0 %collective-permute-done.2 = f32[1,256,768]{2,1,0:T(8,128)} collective-permute-done((f32[1,256,768]{2,1,0:T(8,128)S(1)}, f32[1,256,768]{2,1,0:T(8,128)}, u32[]{:S(2)}, u32[]{:S(2)}) %collective-permute-start.2) | collective-permute-done | bytes 786464 | tf_op jit(solution)/shard_map/ppermute | solution.py:31
  74.9 15.7 %fusion.65 = f32[1,256,3,384]{3,1,2,0:T(8,128)S(1)} fusion(f32[2,768,3,384]{3,1,2,0:T(8,128)} %param.16, f32[1,256,768]{2,1,0:T(8,128)S(1)} %get-tuple-element.127, f32[768]{0:T(1024)S(1)} %copy-done.114, f32[768]{0:T(1024)S(1)} %copy-done.96, f32[256]{0:T(256)S(1)} %fusion.180, f32[256]{0:T(256)S(1)} %broadcast_multiply_fusion.1), kind=kOutput, calls=%fused_computation.81 | convolution fusion | flops 1359740928 | bytes 5513216 | tf_op jit(solution)/shard_map/bsd,dcm->bscm/dot_general | solution.py:127
  102.2 21.9 %all-gather.2 = f32[16,1,768]{2,1,0:T(1,128)S(1)} all-gather(f32[1,1,768]{2,1,0:T(1,128)} %get-tuple-element.100), channel_id=1, replica_groups=mesh['dp'=16,'tensor'=2] {'dp'}, dimensions={0}, use_global_device_ids=true | all-gather | bytes 52224 | tf_op jit(solution)/shard_map/all_gather | solution.py:119
  126.3 4.9 fusion.43
  131.3 6.3 %fusion.206 = (f32[1536]{0:T(1024)}, f32[256,1536]{1,0:T(8,128)S(1)}) fusion(f32[256,1536]{1,0:T(8,128)S(1)} %fusion.43, f32[2,1536,768]{2,1,0:T(8,128)} %param.22, f32[1,256,768]{2,1,0:T(8,128)S(1)} %copy-done.64, f32[768]{0:T(1024)S(1)} %copy-done.154), kind=kOutput, calls=%fused_computation.396 | convolution fusion | flops 1819998720 | bytes 8659968 | tf_op jit(solution)/shard_map/bsd,fd->bsf/dot_general | solution.py:198
  137.7 3.2 fusion.80
  142.9 5.6 fusion.83
  150.5 11.1 %collective-permute-done.5 = f32[1,256,768]{2,1,0:T(8,128)} collective-permute-done((f32[1,256,768]{2,1,0:T(8,128)}, f32[1,256,768]{2,1,0:T(8,128)}, u32[]{:S(2)}, u32[]{:S(2)}) %collective-permute-start.5) | collective-permute-done | bytes 786464 | tf_op jit(solution)/shard_map/ppermute | solution.py:31
  163.9 13.8 %collective-permute-done.4 = f32[1,256,768]{2,1,0:T(8,128)S(1)} collective-permute-done((f32[1,256,768]{2,1,0:T(8,128)S(1)}, f32[1,256,768]{2,1,0:T(8,128)S(1)}, u32[]{:S(2)}, u32[]{:S(2)}) %collective-permute-start.4) | collective-permute-done | bytes 786464 | tf_op jit(solution)/shard_map/ppermute | solution.py:31
  177.8 2.6 multiply_reduce_fusion.19
  191.5 4.7 fusion.71
  201.9 2.9 fusion.187
  218.9 2.6 fusion.215
  227.5 3.1 multiply_reduce_fusion.18
  230.6 6.0 %fusion.207 = (f32[1536]{0:T(1024)}, f32[256,1536]{1,0:T(8,128)S(1)}) fusion(f32[256,1536]{1,0:T(8,128)S(1)} %copy-done.7, f32[2,1536,768]{2,1,0:T(8,128)} %param.22, f32[1,256,768]{2,1,0:T(8,128)S(1)} %get-tuple-element.168, f32[768]{0:T(1024)S(1)} %copy-done.92), kind=kOutput, calls=%fused_computation.397 | convolution fusion | flops 1819998720 | bytes 8659968 | tf_op jit(solution)/shard_map/bsd,fd->bsf/dot_general | solution.py:198
  236.7 3.2 fusion.74
  246.0 21.6 %all-gather.1 = f32[16,1,6528]{2,1,0:T(1,128)} all-gather(f32[1,1,6528]{2,1,0:T(1,128)S(1)} %maximum_bitcast_fusion.1), channel_id=1, replica_groups=mesh['dp'=16,'tensor'=2] {'dp'}, dimensions={0}, use_global_device_ids=true | all-gather | bytes 443904 | tf_op jit(solution)/shard_map/all_gather | solution.py:253
  273.8 2.9 fusion.186
  288.4 3.0 collective-permute-done.24
  293.6 5.0 collective-permute-done.25
  303.2 3.0 multiply_reduce_fusion.17
  312.0 4.8 fusion.68
  330.7 5.6 collective-permute-done.8
  341.4 18.7 %all-gather = f32[16,1,6528]{2,1,0:T(1,128)S(1)} all-gather(f32[1,1,6528]{2,1,0:T(1,128)S(1)} %maximum_bitcast_fusion), channel_id=1, replica_groups=mesh['dp'=16,'tensor'=2] {'dp'}, dimensions={0}, use_global_device_ids=true | all-gather | bytes 443904 | tf_op jit(solution)/shard_map/all_gather | solution.py:253
  361.2 5.9 %fusion.3 = (f32[768]{0:T(1024)S(1)}, f32[768]{0:T(1024)S(1)}) fusion(f32[2,768,2304]{2,1,0:T(8,128)} %param.24, f32[2304]{0:T(1024)S(1)} %get-tuple-element.110, f32[2304]{0:T(1024)S(1)} %copy-done.100), kind=kLoop, calls=%fused_computation.7 | loop fusion | flops 7076352 | bytes 14180352 | tf_op jit(solution)/shard_map/reduce_sum | solution.py:53
  378.7 3.3 convolution_add_fusion.2
  383.4 2.9 convolution_add_fusion.4
  391.0 2.9 collective-permute-done.20
  394.1 5.7 collective-permute-done.21
  402.5 3.2 convolution_add_fusion.3
  405.8 29.7 %collective-permute-done.15 = f32[4,48,1152]{2,1,0:T(8,128)S(1)} collective-permute-done((f32[4,48,1152]{2,1,0:T(8,128)S(1)}, f32[4,48,1152]{2,1,0:T(8,128)S(1)}, u32[]{:S(2)}, u32[]{:S(2)}) %collective-permute-start.15) | collective-permute-done | bytes 884768 | tf_op jit(solution)/shard_map/ppermute | solution.py:87
  436.5 24.4 %collective-permute-done.31 = f32[4,48,1536]{2,1,0:T(8,128)S(1)} collective-permute-done((f32[4,48,1536]{2,1,0:T(8,128)S(1)}, f32[4,48,1536]{2,1,0:T(8,128)S(1)}, u32[]{:S(2)}, u32[]{:S(2)}) %collective-permute-start.31) | collective-permute-done | bytes 1179680 | tf_op jit(solution)/shard_map/ppermute | solution.py:87
  463.3 2.9 convolution_add_fusion.5
  466.3 23.2 %collective-permute-done.17 = f32[1,48,1152]{2,1,0:T(8,128)S(1)} collective-permute-done((f32[1,48,1152]{2,1,0:T(8,128)S(1)}, f32[1,48,1152]{2,1,0:T(8,128)S(1)}, u32[]{:S(2)}, u32[]{:S(2)}) %collective-permute-start.17) | collective-permute-done | bytes 221216 | tf_op jit(solution)/shard_map/ppermute | solution.py:87
  490.2 3.5 collective-permute-start.41
  497.9 13.5 %collective-permute-done.41 = f32[1,48,1536]{2,1,0:T(8,128)S(1)} collective-permute-done((f32[1,48,1536]{2,1,0:T(8,128)S(1)}, f32[1,48,1536]{2,1,0:T(8,128)S(1)}, u32[]{:S(2)}, u32[]{:S(2)}) %collective-permute-start.41) | collective-permute-done | bytes 294944 | tf_op jit(solution)/shard_map/ppermute | solution.py:87
  511.4 5.5 collective-permute-done.33
  517.0 3.6 collective-permute-done.36
  520.7 13.3 %collective-permute-done.11 = f32[4,48,1152]{2,1,0:T(8,128)S(1)} collective-permute-done((f32[4,48,1152]{2,1,0:T(8,128)S(1)}, f32[4,48,1152]{2,1,0:T(8,128)S(1)}, u32[]{:S(2)}, u32[]{:S(2)}) %collective-permute-start.11) | collective-permute-done | bytes 884768 | tf_op jit(solution)/shard_map/ppermute | solution.py:87
  537.4 12.3 %collective-permute-done.12 = f32[2,48,1152]{2,1,0:T(8,128)S(1)} collective-permute-done((f32[2,48,1152]{2,1,0:T(8,128)S(1)}, f32[2,48,1152]{2,1,0:T(8,128)S(1)}, u32[]{:S(2)}, u32[]{:S(2)}) %collective-permute-start.12) | collective-permute-done | bytes 442400 | tf_op jit(solution)/shard_map/ppermute | solution.py:87
  550.6 11.2 %collective-permute-done.28 = f32[2,48,1536]{2,1,0:T(8,128)S(1)} collective-permute-done((f32[2,48,1536]{2,1,0:T(8,128)S(1)}, f32[2,48,1536]{2,1,0:T(8,128)S(1)}, u32[]{:S(2)}, u32[]{:S(2)}) %collective-permute-start.28) | collective-permute-done | bytes 589856 | tf_op jit(solution)/shard_map/ppermute | solution.py:87
  564.1 9.4 %collective-permute-done.29 = f32[1,48,1536]{2,1,0:T(8,128)S(1)} collective-permute-done((f32[1,48,1536]{2,1,0:T(8,128)S(1)}, f32[1,48,1536]{2,1,0:T(8,128)S(1)}, u32[]{:S(2)}, u32[]{:S(2)}) %collective-permute-start.29) | collective-permute-done | bytes 294944 | tf_op jit(solution)/shard_map/ppermute | solution.py:87
  (657 shorter events, 170.7 us)
Async XLA Ops:
  8.6 4.8 collective-permute-start
  14.3 28.2 %copy-start.84 = (f32[768]{0:T(1024)}, f32[768]{0:T(1024)S(1)}, u32[]{:S(2)}) copy-start(f32[768]{0:T(1024)S(1)} %get-tuple-element.190) | copy-start | bytes 9220
  14.3 58.4 %copy-start.91 = (f32[768]{0:T(1024)}, f32[768]{0:T(1024)S(1)}, u32[]{:S(2)}) copy-start(f32[768]{0:T(1024)S(1)} %get-tuple-element.193) | copy-start | bytes 9220
  23.4 19.1 %collective-permute-start.1 = (f32[1,256,768]{2,1,0:T(8,128)S(1)}, f32[1,256,768]{2,1,0:T(8,128)S(1)}, u32[]{:S(2)}, u32[]{:S(2)}) collective-permute-start(f32[1,256,768]{2,1,0:T(8,128)S(1)} %convolution_bitcast_fusion.3), channel_id=1, source_target_pairs={{0,1},{1,0},{2,3},{3,2},{4,5},{5,4},{6,7},{7,6},{8,9},{9,8},{10,11... | collective-permute-start | bytes 2359304 | tf_op jit(solution)/shard_map/ppermute | solution.py:31
  43.4 29.3 %copy-start.2 = (f32[1,256,768]{2,1,0:T(8,128)}, f32[1,256,768]{2,1,0:T(8,128)S(1)}, u32[]{:S(2)}) copy-start(f32[1,256,768]{2,1,0:T(8,128)S(1)} %get-tuple-element.129) | copy-start | bytes 2359300
  54.4 18.3 %collective-permute-start.2 = (f32[1,256,768]{2,1,0:T(8,128)S(1)}, f32[1,256,768]{2,1,0:T(8,128)}, u32[]{:S(2)}, u32[]{:S(2)}) collective-permute-start(f32[1,256,768]{2,1,0:T(8,128)S(1)} %fusion.77), channel_id=1, source_target_pairs={{0,1},{1,0},{2,3},{3,2},{4,5},{5,4},{6,7},{7,6},{8,9},{9,8},{10,11... | collective-permute-start | bytes 2359304 | tf_op jit(solution)/shard_map/ppermute | solution.py:31
  101.9 22.2 %collective-permute-start.3 = (f32[1,256,768]{2,1,0:T(8,128)}, f32[1,256,768]{2,1,0:T(8,128)}, u32[]{:S(2)}, u32[]{:S(2)}) collective-permute-start(f32[1,256,768]{2,1,0:T(8,128)} %convolution_bitcast_fusion.2), channel_id=1, source_target_pairs={{0,1},{1,0},{2,3},{3,2},{4,5},{5,4},{6,7},{7,6},{8,9},{9,8},{10,11... | collective-permute-start | bytes 2359304 | tf_op jit(solution)/shard_map/ppermute | solution.py:31
  140.9 20.7 %collective-permute-start.5 = (f32[1,256,768]{2,1,0:T(8,128)}, f32[1,256,768]{2,1,0:T(8,128)}, u32[]{:S(2)}, u32[]{:S(2)}) collective-permute-start(f32[1,256,768]{2,1,0:T(8,128)} %fusion.80), channel_id=1, source_target_pairs={{0,1},{1,0},{2,3},{3,2},{4,5},{5,4},{6,7},{7,6},{8,9},{9,8},{10,11... | collective-permute-start | bytes 2359304 | tf_op jit(solution)/shard_map/ppermute | solution.py:31
  148.5 29.3 %collective-permute-start.4 = (f32[1,256,768]{2,1,0:T(8,128)S(1)}, f32[1,256,768]{2,1,0:T(8,128)S(1)}, u32[]{:S(2)}, u32[]{:S(2)}) collective-permute-start(f32[1,256,768]{2,1,0:T(8,128)S(1)} %fusion.83), channel_id=1, source_target_pairs={{0,1},{1,0},{2,3},{3,2},{4,5},{5,4},{6,7},{7,6},{8,9},{9,8},{10,11... | collective-permute-start | bytes 2359304 | tf_op jit(solution)/shard_map/ppermute | solution.py:31
  150.5 27.3 %copy-start.117 = (f32[768]{0:T(1024)S(1)}, f32[768]{0:T(1024)}, u32[]{:S(2)}) copy-start(f32[768]{0:T(1024)} %get-tuple-element.79) | copy-start | bytes 9220
  150.5 27.3 %copy-start.145 = (f32[768]{0:T(1024)S(1)}, f32[768]{0:T(1024)}, u32[]{:S(2)}) copy-start(f32[768]{0:T(1024)} %get-tuple-element.92) | copy-start | bytes 9220
  150.5 27.3 %copy-start.155 = (f32[768]{0:T(1024)S(1)}, f32[768]{0:T(1024)}, u32[]{:S(2)}) copy-start(f32[768]{0:T(1024)} %get-tuple-element.80) | copy-start | bytes 9220
  196.2 27.9 %collective-permute-start.6 = (f32[1,256,768]{2,1,0:T(8,128)}, f32[1,256,768]{2,1,0:T(8,128)}, u32[]{:S(2)}, u32[]{:S(2)}) collective-permute-start(f32[1,256,768]{2,1,0:T(8,128)} %fusion.71), channel_id=1, source_target_pairs={{0,1},{1,0},{2,3},{3,2},{4,5},{5,4},{6,7},{7,6},{8,9},{9,8},{10,11... | collective-permute-start | bytes 2359304 | tf_op jit(solution)/shard_map/ppermute | solution.py:31
  210.5 11.1 %collective-permute-start.22 = (f32[384,384]{1,0:T(8,128)}, f32[384,384]{1,0:T(8,128)}, u32[]{:S(2)}, u32[]{:S(2)}) collective-permute-start(f32[384,384]{1,0:T(8,128)} %fusion.213), channel_id=1, source_target_pairs={{0,2},{2,0},{4,6},{6,4},{8,10},{10,8},{12,14},{14,12},{16,18},{18,... | collective-permute-start | bytes 1769480 | tf_op jit(solution)/shard_map/ppermute | solution.py:77
  214.0 163.1 %collective-permute-start.38 = (f32[384,1536]{1,0:T(8,128)}, f32[384,1536]{1,0:T(8,128)}, u32[]{:S(2)}, u32[]{:S(2)}) collective-permute-start(f32[384,1536]{1,0:T(8,128)} %fusion.187), channel_id=1, source_target_pairs={{0,2},{2,0},{4,6},{6,4},{8,10},{10,8},{12,14},{14,12},{16,18},{18,... | collective-permute-start | bytes 7077896 | tf_op jit(solution)/shard_map/ppermute | solution.py:77
  221.5 160.6 %collective-permute-start.30 = (f32[384,1536]{1,0:T(8,128)}, f32[384,1536]{1,0:T(8,128)}, u32[]{:S(2)}, u32[]{:S(2)}) collective-permute-start(f32[384,1536]{1,0:T(8,128)} %fusion.215), channel_id=1, source_target_pairs={{0,2},{2,0},{4,6},{6,4},{8,10},{10,8},{12,14},{14,12},{16,18},{18,... | collective-permute-start | bytes 7077896 | tf_op jit(solution)/shard_map/ppermute | solution.py:77
  224.1 59.1 %collective-permute-start.23 = (f32[4,48,384]{2,1,0:T(8,128)}, f32[4,48,384]{2,1,0:T(8,128)}, u32[]{:S(2)}, u32[]{:S(2)}) collective-permute-start(f32[4,48,384]{2,1,0:T(8,128)} %dynamic-slice_bitcast_fusion.12), channel_id=1, source_target_pairs={{0,4},{2,6},{4,0},{6,2},{8,12},{10,14},{12,8},{14,10},{16,20},{18,... | collective-permute-start | bytes 884744 | tf_op jit(solution)/shard_map/ppermute | solution.py:87
  240.0 59.3 %collective-permute-start.7 = (f32[1,256,768]{2,1,0:T(8,128)}, f32[1,256,768]{2,1,0:T(8,128)}, u32[]{:S(2)}, u32[]{:S(2)}) collective-permute-start(f32[1,256,768]{2,1,0:T(8,128)} %fusion.74), channel_id=1, source_target_pairs={{0,1},{1,0},{2,3},{3,2},{4,5},{5,4},{6,7},{7,6},{8,9},{9,8},{10,11... | collective-permute-start | bytes 2359304 | tf_op jit(solution)/shard_map/ppermute | solution.py:31
  285.0 6.4 %collective-permute-start.24 = (f32[2,48,384]{2,1,0:T(8,128)}, f32[2,48,384]{2,1,0:T(8,128)}, u32[]{:S(2)}, u32[]{:S(2)}) collective-permute-start(f32[2,48,384]{2,1,0:T(8,128)} %dynamic-slice_bitcast_fusion.14), channel_id=1, source_target_pairs={{0,8},{2,10},{4,12},{6,14},{8,0},{10,2},{12,4},{14,6},{16,24},{18,... | collective-permute-start | bytes 442376 | tf_op jit(solution)/shard_map/ppermute | solution.py:87
  286.3 115.7 %collective-permute-start.34 = (f32[384,1536]{1,0:T(8,128)}, f32[384,1536]{1,0:T(8,128)}, u32[]{:S(2)}, u32[]{:S(2)}) collective-permute-start(f32[384,1536]{1,0:T(8,128)} %fusion.186), channel_id=1, source_target_pairs={{0,2},{2,0},{4,6},{6,4},{8,10},{10,8},{12,14},{14,12},{16,18},{18,... | collective-permute-start | bytes 7077896 | tf_op jit(solution)/shard_map/ppermute | solution.py:77
  292.3 6.3 %collective-permute-start.25 = (f32[1,48,384]{2,1,0:T(8,128)S(1)}, f32[1,48,384]{2,1,0:T(8,128)S(1)}, u32[]{:S(2)}, u32[]{:S(2)}) collective-permute-start(f32[1,48,384]{2,1,0:T(8,128)S(1)} %constant_dynamic-slice_fusion.13), channel_id=1, source_target_pairs={{0,16},{2,18},{4,20},{6,22},{8,24},{10,26},{12,28},{14,30},{16,0},... | collective-permute-start | bytes 221192 | tf_op jit(solution)/shard_map/ppermute | solution.py:87
  316.8 19.5 %collective-permute-start.8 = (f32[1,256,768]{2,1,0:T(8,128)}, f32[1,256,768]{2,1,0:T(8,128)}, u32[]{:S(2)}, u32[]{:S(2)}) collective-permute-start(f32[1,256,768]{2,1,0:T(8,128)} %fusion.68), channel_id=1, source_target_pairs={{0,1},{1,0},{2,3},{3,2},{4,5},{5,4},{6,7},{7,6},{8,9},{9,8},{10,11... | collective-permute-start | bytes 2359304 | tf_op jit(solution)/shard_map/ppermute | solution.py:31
  322.0 6.5 %collective-permute-start.18 = (f32[384,384]{1,0:T(8,128)}, f32[384,384]{1,0:T(8,128)}, u32[]{:S(2)}, u32[]{:S(2)}) collective-permute-start(f32[384,384]{1,0:T(8,128)} %fusion.212), channel_id=1, source_target_pairs={{0,2},{2,0},{4,6},{6,4},{8,10},{10,8},{12,14},{14,12},{16,18},{18,... | collective-permute-start | bytes 1769480 | tf_op jit(solution)/shard_map/ppermute | solution.py:77
  328.5 59.8 %collective-permute-start.14 = (f32[384,1152]{1,0:T(8,128)}, f32[384,1152]{1,0:T(8,128)}, u32[]{:S(2)}, u32[]{:S(2)}) collective-permute-start(f32[384,1152]{1,0:T(8,128)} %fusion.211), channel_id=1, source_target_pairs={{0,2},{2,0},{4,6},{6,4},{8,10},{10,8},{12,14},{14,12},{16,18},{18,... | collective-permute-start | bytes 5308424 | tf_op jit(solution)/shard_map/ppermute | solution.py:77
  336.2 127.0 %collective-permute-start.26 = (f32[384,1536]{1,0:T(8,128)}, f32[384,1536]{1,0:T(8,128)}, u32[]{:S(2)}, u32[]{:S(2)}) collective-permute-start(f32[384,1536]{1,0:T(8,128)} %fusion.214), channel_id=1, source_target_pairs={{0,2},{2,0},{4,6},{6,4},{8,10},{10,8},{12,14},{14,12},{16,18},{18,... | collective-permute-start | bytes 7077896 | tf_op jit(solution)/shard_map/ppermute | solution.py:77
  377.2 10.6 %collective-permute-start.19 = (f32[4,48,384]{2,1,0:T(8,128)S(1)}, f32[4,48,384]{2,1,0:T(8,128)S(1)}, u32[]{:S(2)}, u32[]{:S(2)}) collective-permute-start(f32[4,48,384]{2,1,0:T(8,128)S(1)} %dynamic-slice_bitcast_fusion.13), channel_id=1, source_target_pairs={{0,4},{2,6},{4,0},{6,2},{8,12},{10,14},{12,8},{14,10},{16,20},{18,... | collective-permute-start | bytes 884744 | tf_op jit(solution)/shard_map/ppermute | solution.py:87
  382.1 4.5 collective-permute-start.9
  386.6 107.3 %collective-permute-start.10 = (f32[384,1152]{1,0:T(8,128)S(1)}, f32[384,1152]{1,0:T(8,128)S(1)}, u32[]{:S(2)}, u32[]{:S(2)}) collective-permute-start(f32[384,1152]{1,0:T(8,128)S(1)} %fusion.210), channel_id=1, source_target_pairs={{0,2},{2,0},{4,6},{6,4},{8,10},{10,8},{12,14},{14,12},{16,18},{18,... | collective-permute-start | bytes 5308424 | tf_op jit(solution)/shard_map/ppermute | solution.py:77
  387.7 48.4 %collective-permute-start.39 = (f32[4,48,1536]{2,1,0:T(8,128)S(1)}, f32[4,48,1536]{2,1,0:T(8,128)S(1)}, u32[]{:S(2)}, u32[]{:S(2)}) collective-permute-start(f32[4,48,1536]{2,1,0:T(8,128)S(1)} %dynamic-slice_bitcast_fusion), channel_id=1, source_target_pairs={{0,4},{2,6},{4,0},{6,2},{8,12},{10,14},{12,8},{14,10},{16,20},{18,... | collective-permute-start | bytes 3538952 | tf_op jit(solution)/shard_map/ppermute | solution.py:87
  388.3 5.6 collective-permute-start.20
  393.9 5.8 %collective-permute-start.21 = (f32[1,48,384]{2,1,0:T(8,128)S(1)}, f32[1,48,384]{2,1,0:T(8,128)S(1)}, u32[]{:S(2)}, u32[]{:S(2)}) collective-permute-start(f32[1,48,384]{2,1,0:T(8,128)S(1)} %constant_dynamic-slice_fusion.16), channel_id=1, source_target_pairs={{0,16},{2,18},{4,20},{6,22},{8,24},{10,26},{12,28},{14,30},{16,0},... | collective-permute-start | bytes 221192 | tf_op jit(solution)/shard_map/ppermute | solution.py:87
  399.8 35.8 %collective-permute-start.15 = (f32[4,48,1152]{2,1,0:T(8,128)S(1)}, f32[4,48,1152]{2,1,0:T(8,128)S(1)}, u32[]{:S(2)}, u32[]{:S(2)}) collective-permute-start(f32[4,48,1152]{2,1,0:T(8,128)S(1)} %dynamic-slice_bitcast_fusion.4), channel_id=1, source_target_pairs={{0,4},{2,6},{4,0},{6,2},{8,12},{10,14},{12,8},{14,10},{16,20},{18,... | collective-permute-start | bytes 2654216 | tf_op jit(solution)/shard_map/ppermute | solution.py:87
  402.0 58.8 %collective-permute-start.31 = (f32[4,48,1536]{2,1,0:T(8,128)S(1)}, f32[4,48,1536]{2,1,0:T(8,128)S(1)}, u32[]{:S(2)}, u32[]{:S(2)}) collective-permute-start(f32[4,48,1536]{2,1,0:T(8,128)S(1)} %dynamic-slice_bitcast_fusion.2), channel_id=1, source_target_pairs={{0,4},{2,6},{4,0},{6,2},{8,12},{10,14},{12,8},{14,10},{16,20},{18,... | collective-permute-start | bytes 3538952 | tf_op jit(solution)/shard_map/ppermute | solution.py:87
  435.5 61.1 %collective-permute-start.35 = (f32[4,48,1536]{2,1,0:T(8,128)S(1)}, f32[4,48,1536]{2,1,0:T(8,128)S(1)}, u32[]{:S(2)}, u32[]{:S(2)}) collective-permute-start(f32[4,48,1536]{2,1,0:T(8,128)S(1)} %dynamic-slice_bitcast_fusion.1), channel_id=1, source_target_pairs={{0,4},{2,6},{4,0},{6,2},{8,12},{10,14},{12,8},{14,10},{16,20},{18,... | collective-permute-start | bytes 3538952 | tf_op jit(solution)/shard_map/ppermute | solution.py:87
  436.2 24.9 %collective-permute-start.16 = (f32[2,48,1152]{2,1,0:T(8,128)S(1)}, f32[2,48,1152]{2,1,0:T(8,128)S(1)}, u32[]{:S(2)}, u32[]{:S(2)}) collective-permute-start(f32[2,48,1152]{2,1,0:T(8,128)S(1)} %dynamic-slice_bitcast_fusion.10), channel_id=1, source_target_pairs={{0,8},{2,10},{4,12},{6,14},{8,0},{10,2},{12,4},{14,6},{16,24},{18,... | collective-permute-start | bytes 1327112 | tf_op jit(solution)/shard_map/ppermute | solution.py:87
  460.8 29.2 %collective-permute-start.40 = (f32[2,48,1536]{2,1,0:T(8,128)S(1)}, f32[2,48,1536]{2,1,0:T(8,128)S(1)}, u32[]{:S(2)}, u32[]{:S(2)}) collective-permute-start(f32[2,48,1536]{2,1,0:T(8,128)S(1)} %dynamic-slice_bitcast_fusion.6), channel_id=1, source_target_pairs={{0,8},{2,10},{4,12},{6,14},{8,0},{10,2},{12,4},{14,6},{16,24},{18,... | collective-permute-start | bytes 1769480 | tf_op jit(solution)/shard_map/ppermute | solution.py:87
  461.0 32.7 %collective-permute-start.32 = (f32[2,48,1536]{2,1,0:T(8,128)S(1)}, f32[2,48,1536]{2,1,0:T(8,128)S(1)}, u32[]{:S(2)}, u32[]{:S(2)}) collective-permute-start(f32[2,48,1536]{2,1,0:T(8,128)S(1)} %dynamic-slice_bitcast_fusion.8), channel_id=1, source_target_pairs={{0,8},{2,10},{4,12},{6,14},{8,0},{10,2},{12,4},{14,6},{16,24},{18,... | collective-permute-start | bytes 1769480 | tf_op jit(solution)/shard_map/ppermute | solution.py:87
  463.2 26.3 %collective-permute-start.17 = (f32[1,48,1152]{2,1,0:T(8,128)S(1)}, f32[1,48,1152]{2,1,0:T(8,128)S(1)}, u32[]{:S(2)}, u32[]{:S(2)}) collective-permute-start(f32[1,48,1152]{2,1,0:T(8,128)S(1)} %constant_dynamic-slice_fusion.19), channel_id=1, source_target_pairs={{0,16},{2,18},{4,20},{6,22},{8,24},{10,26},{12,28},{14,30},{16,0},... | collective-permute-start | bytes 663560 | tf_op jit(solution)/shard_map/ppermute | solution.py:87
  489.5 46.0 %collective-permute-start.27 = (f32[4,48,1536]{2,1,0:T(8,128)S(1)}, f32[4,48,1536]{2,1,0:T(8,128)S(1)}, u32[]{:S(2)}, u32[]{:S(2)}) collective-permute-start(f32[4,48,1536]{2,1,0:T(8,128)S(1)} %dynamic-slice_bitcast_fusion.3), channel_id=1, source_target_pairs={{0,4},{2,6},{4,0},{6,2},{8,12},{10,14},{12,8},{14,10},{16,20},{18,... | collective-permute-start | bytes 3538952 | tf_op jit(solution)/shard_map/ppermute | solution.py:87
  490.2 21.2 %collective-permute-start.41 = (f32[1,48,1536]{2,1,0:T(8,128)S(1)}, f32[1,48,1536]{2,1,0:T(8,128)S(1)}, u32[]{:S(2)}, u32[]{:S(2)}) collective-permute-start(f32[1,48,1536]{2,1,0:T(8,128)S(1)} %constant_dynamic-slice_fusion.1), channel_id=1, source_target_pairs={{0,16},{2,18},{4,20},{6,22},{8,24},{10,26},{12,28},{14,30},{16,0},... | collective-permute-start | bytes 884744 | tf_op jit(solution)/shard_map/ppermute | solution.py:87
  493.8 23.1 %collective-permute-start.33 = (f32[1,48,1536]{2,1,0:T(8,128)S(1)}, f32[1,48,1536]{2,1,0:T(8,128)S(1)}, u32[]{:S(2)}, u32[]{:S(2)}) collective-permute-start(f32[1,48,1536]{2,1,0:T(8,128)S(1)} %constant_dynamic-slice_fusion.7), channel_id=1, source_target_pairs={{0,16},{2,18},{4,20},{6,22},{8,24},{10,26},{12,28},{14,30},{16,0},... | collective-permute-start | bytes 884744 | tf_op jit(solution)/shard_map/ppermute | solution.py:87
  495.0 39.0 %collective-permute-start.11 = (f32[4,48,1152]{2,1,0:T(8,128)S(1)}, f32[4,48,1152]{2,1,0:T(8,128)S(1)}, u32[]{:S(2)}, u32[]{:S(2)}) collective-permute-start(f32[4,48,1152]{2,1,0:T(8,128)S(1)} %dynamic-slice_bitcast_fusion.5), channel_id=1, source_target_pairs={{0,4},{2,6},{4,0},{6,2},{8,12},{10,14},{12,8},{14,10},{16,20},{18,... | collective-permute-start | bytes 2654216 | tf_op jit(solution)/shard_map/ppermute | solution.py:87
  496.8 23.7 %collective-permute-start.36 = (f32[2,48,1536]{2,1,0:T(8,128)S(1)}, f32[2,48,1536]{2,1,0:T(8,128)S(1)}, u32[]{:S(2)}, u32[]{:S(2)}) collective-permute-start(f32[2,48,1536]{2,1,0:T(8,128)S(1)} %dynamic-slice_bitcast_fusion.7), channel_id=1, source_target_pairs={{0,8},{2,10},{4,12},{6,14},{8,0},{10,2},{12,4},{14,6},{16,24},{18,... | collective-permute-start | bytes 1769480 | tf_op jit(solution)/shard_map/ppermute | solution.py:87
  520.7 15.8 %collective-permute-start.37 = (f32[1,48,1536]{2,1,0:T(8,128)S(1)}, f32[1,48,1536]{2,1,0:T(8,128)S(1)}, u32[]{:S(2)}, u32[]{:S(2)}) collective-permute-start(f32[1,48,1536]{2,1,0:T(8,128)S(1)} %constant_dynamic-slice_fusion.4), channel_id=1, source_target_pairs={{0,16},{2,18},{4,20},{6,22},{8,24},{10,26},{12,28},{14,30},{16,0},... | collective-permute-start | bytes 884744 | tf_op jit(solution)/shard_map/ppermute | solution.py:87
  534.1 15.5 %collective-permute-start.12 = (f32[2,48,1152]{2,1,0:T(8,128)S(1)}, f32[2,48,1152]{2,1,0:T(8,128)S(1)}, u32[]{:S(2)}, u32[]{:S(2)}) collective-permute-start(f32[2,48,1152]{2,1,0:T(8,128)S(1)} %dynamic-slice_bitcast_fusion.11), channel_id=1, source_target_pairs={{0,8},{2,10},{4,12},{6,14},{8,0},{10,2},{12,4},{14,6},{16,24},{18,... | collective-permute-start | bytes 1327112 | tf_op jit(solution)/shard_map/ppermute | solution.py:87
  535.7 26.0 %collective-permute-start.28 = (f32[2,48,1536]{2,1,0:T(8,128)S(1)}, f32[2,48,1536]{2,1,0:T(8,128)S(1)}, u32[]{:S(2)}, u32[]{:S(2)}) collective-permute-start(f32[2,48,1536]{2,1,0:T(8,128)S(1)} %dynamic-slice_bitcast_fusion.9), channel_id=1, source_target_pairs={{0,8},{2,10},{4,12},{6,14},{8,0},{10,2},{12,4},{14,6},{16,24},{18,... | collective-permute-start | bytes 1769480 | tf_op jit(solution)/shard_map/ppermute | solution.py:87
  549.8 13.4 %collective-permute-start.13 = (f32[1,48,1152]{2,1,0:T(8,128)S(1)}, f32[1,48,1152]{2,1,0:T(8,128)S(1)}, u32[]{:S(2)}, u32[]{:S(2)}) collective-permute-start(f32[1,48,1152]{2,1,0:T(8,128)S(1)} %constant_dynamic-slice_fusion.22), channel_id=1, source_target_pairs={{0,16},{2,18},{4,20},{6,22},{8,24},{10,26},{12,28},{14,30},{16,0},... | collective-permute-start | bytes 663560 | tf_op jit(solution)/shard_map/ppermute | solution.py:87
  561.8 11.6 %collective-permute-start.29 = (f32[1,48,1536]{2,1,0:T(8,128)S(1)}, f32[1,48,1536]{2,1,0:T(8,128)S(1)}, u32[]{:S(2)}, u32[]{:S(2)}) collective-permute-start(f32[1,48,1536]{2,1,0:T(8,128)S(1)} %constant_dynamic-slice_fusion.10), channel_id=1, source_target_pairs={{0,16},{2,18},{4,20},{6,22},{8,24},{10,26},{12,28},{14,30},{16,0},... | collective-permute-start | bytes 884744 | tf_op jit(solution)/shard_map/ppermute | solution.py:87
  (176 other events, 862.7 us)
